TPU v7x, 512 devices: a whole 4x8x8 slice. The times are simulated.
512 devices in a mesh: blk: 8 (over y_lo, core), leaf: 64 (over z, y_hi, x).
Axes of the slice: x: 4, y: 8 (y_hi: 2, y_lo: 4; y = y_hi * 4 + y_lo), z: 8, core: 2. Of those that a mesh axis runs over, the one named last changes fastest.
Arguments:
- positions: float32 [3, 64, 8, 128], P(None, 'leaf', 'blk'), may hold values from 0 to 32, as said below
- panel_areas: float32 [64, 8, 128], P('leaf', 'blk'), may hold values from 0.5 to 2
- probe_cols: bfloat16 [576, 64, 8, 128], P(None, 'leaf', 'blk'), may hold values from -5 to 5
- full_sketch: bfloat16 [576, 64, 8, 128], P(None, 'leaf', 'blk'), may hold values from -3 to 3
- tree_order: int32 [64, 8, 128], P('leaf', 'blk'), may hold values from 0 to 127, each once within a row
- leaf_basis: bfloat16 [64, 8, 128, 512], P('leaf', 'blk'), may hold values from -0.1875 to 0.1875
- transfer_mats: bfloat16 [64, 3, 512, 512], P('leaf'), may hold values from -0.1875 to 0.1875
Outputs:
- offdiag_sketch: bfloat16 [576, 64, 8, 128], P(None, 'leaf', 'blk')
- nested_sketch: float32 [64, 2, 576, 512], P('leaf')
Inputs may be any that keep to these rules, and one draw needn't show every extreme that they name: `positions`: each leaf's panel centres lie on a surface patch of 32 by 32 mean panel widths. `tree_order`: along the last dimension, each row names every one of the 128 panels of its block once.
All inputs are finite; a program needn't handle non-finite values.
Results may differ from a plain program's by a relative error of at most 0.0046.
Values sent between devices are 32-bit elements; how exact they have to be, the bound alone decides.
No kernel may reach another device: no remote copies, remote signals or barrier semaphores. Data moves between devices by JAX's collectives and lax.ppermute only.
A program may use at most 64 MiB of HBM per device.

v0:
```python
import math
import jax
import jax.numpy as jnp
from jax import lax
from jax.sharding import PartitionSpec as P

inv_four_pi = 1.0 / (4.0 * math.pi)


def partner(value, axis, bit):
    mask = 2**bit
    pairs = [(source, source ^ mask) for source in range(lax.axis_size(axis))]
    return lax.ppermute(value, axis, pairs)


def kernel_tile(target_pos, target_area, source_pos, source_area):
    distance = jnp.zeros((target_pos.shape[1], source_pos.shape[1]), jnp.float32)
    for component in range(3):
        gap = target_pos[component][:, None] - source_pos[component][None, :]
        distance = distance + gap * gap
    soft = distance + 0.5 * (target_area[:, None] + source_area[None, :])
    return (inv_four_pi * lax.rsqrt(soft)).astype(jnp.bfloat16)


def target_blocks(target_pos, target_area):
    panels = target_pos.shape[1]
    block_size = min(512, panels)
    block_count = panels // block_size
    pos_blocks = jnp.transpose(target_pos.reshape(3, block_count, block_size), (1, 0, 2))
    return (pos_blocks, target_area.reshape(block_count, block_size))


def near_block(target_pos, target_area, source_pos, source_area, source_scaled):
    pos_blocks, area_blocks = target_blocks(target_pos, target_area)

    def one_block(entry):
        block_pos, block_area = entry
        kernel = kernel_tile(block_pos, block_area, source_pos, source_area)
        return lax.dot_general(
            source_scaled, kernel, (((1,), (1,)), ((), ())), preferred_element_type=jnp.float32
        )

    sums = lax.map(one_block, (pos_blocks, area_blocks))
    return jnp.transpose(sums, (1, 0, 2)).reshape(source_scaled.shape[0], target_pos.shape[1])


def project(current, level_mat):
    return jnp.dot(current, level_mat.astype(jnp.float32), precision=lax.Precision.HIGHEST)


def climb_both(sketch, probes, level_mats):
    for tree_level in range(level_mats.shape[0]):
        sketch_proj = project(sketch, level_mats[tree_level])
        probe_proj = project(probes, level_mats[tree_level])
        other_sketch, other_probe = partner((sketch_proj, probe_proj), "leaf", tree_level)
        sketch = sketch_proj + other_sketch
        probes = probe_proj + other_probe
    return (sketch, probes)


def shards(positions, panel_areas, probe_cols, full_sketch, tree_order, leaf_basis, transfer_mats):
    panels = positions.shape[3]
    probe_count = probe_cols.shape[0]
    basis_width = leaf_basis.shape[3]
    level_count = transfer_mats.shape[1]
    coords = positions.reshape(3, panels)
    area_row = panel_areas.reshape(1, panels)
    probe_flat = probe_cols.reshape(probe_count, panels)
    scaled = (area_row * probe_flat.astype(jnp.float32)).astype(jnp.bfloat16)
    sorting = tree_order.reshape(panels)
    basis_flat = leaf_basis.reshape(panels, basis_width)
    level_mats = transfer_mats.reshape(level_count, basis_width, basis_width)
    probe_part = jnp.dot(
        jnp.take(probe_flat, sorting, axis=1), basis_flat, preferred_element_type=jnp.float32
    )
    outgoing = jnp.concatenate([coords, area_row, scaled.astype(jnp.float32)], axis=0)
    piece = lax.all_gather(outgoing, "blk", axis=1, tiled=True)
    near_sum = near_block(coords, area_row[0], piece[:3], piece[3], piece[4:].astype(jnp.bfloat16))
    offdiag = (full_sketch.reshape(probe_count, panels).astype(jnp.float32) - near_sum).astype(
        jnp.bfloat16
    )
    sketch_part = jnp.dot(
        jnp.take(offdiag, sorting, axis=1), basis_flat, preferred_element_type=jnp.float32
    )
    sketch_sum, probe_sum = lax.psum((sketch_part, probe_part), "blk")
    sketch_top, probe_top = climb_both(sketch_sum, probe_sum, level_mats)
    nested = jnp.stack([sketch_top, probe_top], axis=0)[None]
    return (offdiag.reshape(probe_count, 1, 1, panels), nested)


def solution(mesh):
    in_specs = (
        P(None, "leaf", "blk", None),
        P("leaf", "blk", None),
        P(None, "leaf", "blk", None),
        P(None, "leaf", "blk", None),
        P("leaf", "blk", None),
        P("leaf", "blk", None, None),
        P("leaf", None, None, None),
    )
    out_specs = (P(None, "leaf", "blk", None), P("leaf", None, None, None))
    return jax.shard_map(shards, mesh=mesh, in_specs=in_specs, out_specs=out_specs, check_vma=False)
```

profile of v0, /device:TPU:25, one launch (start us, length us, event | category | flops | bytes accessed | tf_op | source)
XLA Modules:
  0.0 356.3 jit_solution(13410690366226778184)
XLA Ops:
  7.2 0.8 copy.15
  8.0 0.8 copy.13
  8.8 1.1 copy.14
  9.8 0.7 fusion.36
  10.6 0.9 pad_maximum_fusion
  11.6 0.9 gather_fusion.1
  12.6 1.4 fusion.37
  14.0 44.9 %all-gather.2.cloned.1.call-done = f32[580,1024]{0,1:T(8,128)} async-done(((f32[580,128]{0,1:T(8,128)}), f32[580,1024]{0,1:T(8,128)}) %all-gather.2.cloned.1.call-update) | async-done | bytes 2375696 | tf_op jit(solution)/shard_map/all_gather | solution.py:77
  58.9 2.8 slice_reduce_fusion.3
  61.8 3.6 %fusion.23 = (bf16[576,1,1,128]{3,0,2,1:T(8,128)(2,1)}, f32[576,128]{1,0:T(8,128)S(1)}) fusion(bf16[576,1,1,128]{3,0,2,1:T(8,128)(2,1)S(1)} %copy-done.3, f32[1024]{0:T(1024)S(1)} %get-tuple-element.18, f32[128]{0:T(128)S(1)} %bitcast.61, f32[1024]{0:T(1024)S(1)} %get-tuple-element.19, f32[128]{0:T(128)S(1)} %get-tuple-element.31, ...), kind=kOutput, calls=%fused_computation.38 | convolution fusion | flops 152920064 | bytes 1918976 | tf_op jit(solution)/shard_map/while/body/eval_jaxpr/dot_general | solution.py:39
  65.6 0.9 gather_fusion
  66.5 1.4 fusion.39
  67.9 87.3 %all-reduce.3.cloned.1.call-done = (f32[576,512]{1,0:T(8,128)}, f32[576,512]{1,0:T(8,128)}) async-done(((f32[576,512]{1,0:T(8,128)}, f32[576,512]{1,0:T(8,128)}), (f32[576,512]{1,0:T(8,128)}, f32[576,512]{1,0:T(8,128)})) %all-reduce.3.cloned.1.call-update) | async-done | bytes 2359312 | tf_op jit(solution)/shard_map/psum | solution.py:85
  155.2 2.5 fusion.15
  157.7 3.1 collective-permute-start
  160.8 1.1 fusion.13
  161.9 2.2 collective-permute-start.3
  164.1 23.5 %collective-permute-done = f32[576,512]{1,0:T(8,128)S(1)} collective-permute-done((f32[576,512]{1,0:T(8,128)S(1)}, f32[576,512]{1,0:T(8,128)S(1)}, u32[]{:S(2)}, u32[]{:S(2)}) %collective-permute-start) | collective-permute-done | bytes 1179680 | tf_op jit(solution)/shard_map/ppermute | solution.py:13
  187.6 1.1 fusion.7
  188.7 4.6 %collective-permute-start.1 = (f32[576,512]{1,0:T(8,128)S(1)}, f32[576,512]{1,0:T(8,128)S(1)}, u32[]{:S(2)}, u32[]{:S(2)}) collective-permute-start(f32[576,512]{1,0:T(8,128)S(1)} %fusion.7), channel_id=1, source_target_pairs={{0,2},{1,3},{2,0},{3,1},{4,6},{5,7},{6,4},{7,5},{8,10},{9,11},{10,... | collective-permute-start | bytes 3538952 | tf_op jit(solution)/shard_map/ppermute | solution.py:13
  193.3 19.6 %collective-permute-done.3 = f32[576,512]{1,0:T(8,128)S(1)} collective-permute-done((f32[576,512]{1,0:T(8,128)S(1)}, f32[576,512]{1,0:T(8,128)S(1)}, u32[]{:S(2)}, u32[]{:S(2)}) %collective-permute-start.3) | collective-permute-done | bytes 1179680 | tf_op jit(solution)/shard_map/ppermute | solution.py:13
  212.9 1.1 fusion.3
  214.0 4.6 %collective-permute-start.4 = (f32[576,512]{1,0:T(8,128)S(1)}, f32[576,512]{1,0:T(8,128)S(1)}, u32[]{:S(2)}, u32[]{:S(2)}) collective-permute-start(f32[576,512]{1,0:T(8,128)S(1)} %fusion.3), channel_id=1, source_target_pairs={{0,2},{1,3},{2,0},{3,1},{4,6},{5,7},{6,4},{7,5},{8,10},{9,11},{10,... | collective-permute-start | bytes 3538952 | tf_op jit(solution)/shard_map/ppermute | solution.py:13
  218.6 21.7 %collective-permute-done.1 = f32[576,512]{1,0:T(8,128)S(1)} collective-permute-done((f32[576,512]{1,0:T(8,128)S(1)}, f32[576,512]{1,0:T(8,128)S(1)}, u32[]{:S(2)}, u32[]{:S(2)}) %collective-permute-start.1) | collective-permute-done | bytes 1179680 | tf_op jit(solution)/shard_map/ppermute | solution.py:13
  240.3 1.1 fusion.5
  241.4 5.0 %collective-permute-start.2 = (f32[576,512]{1,0:T(8,128)S(1)}, f32[576,512]{1,0:T(8,128)S(1)}, u32[]{:S(2)}, u32[]{:S(2)}) collective-permute-start(f32[576,512]{1,0:T(8,128)S(1)} %fusion.5), channel_id=1, source_target_pairs={{0,4},{1,5},{2,6},{3,7},{4,0},{5,1},{6,2},{7,3},{8,12},{9,13},{10,... | collective-permute-start | bytes 3538952 | tf_op jit(solution)/shard_map/ppermute | solution.py:13
  246.4 17.7 %collective-permute-done.4 = f32[576,512]{1,0:T(8,128)S(1)} collective-permute-done((f32[576,512]{1,0:T(8,128)S(1)}, f32[576,512]{1,0:T(8,128)S(1)}, u32[]{:S(2)}, u32[]{:S(2)}) %collective-permute-start.4) | collective-permute-done | bytes 1179680 | tf_op jit(solution)/shard_map/ppermute | solution.py:13
  264.2 1.1 fusion.1
  265.3 5.2 %collective-permute-start.5 = (f32[576,512]{1,0:T(8,128)S(1)}, f32[576,512]{1,0:T(8,128)S(1)}, u32[]{:S(2)}, u32[]{:S(2)}) collective-permute-start(f32[576,512]{1,0:T(8,128)S(1)} %fusion.1), channel_id=1, source_target_pairs={{0,4},{1,5},{2,6},{3,7},{4,0},{5,1},{6,2},{7,3},{8,12},{9,13},{10,... | collective-permute-start | bytes 3538952 | tf_op jit(solution)/shard_map/ppermute | solution.py:13
  270.5 52.0 %collective-permute-done.2 = f32[576,512]{1,0:T(8,128)S(1)} collective-permute-done((f32[576,512]{1,0:T(8,128)S(1)}, f32[576,512]{1,0:T(8,128)S(1)}, u32[]{:S(2)}, u32[]{:S(2)}) %collective-permute-start.2) | collective-permute-done | bytes 1179680 | tf_op jit(solution)/shard_map/ppermute | solution.py:13
  322.8 24.8 %collective-permute-done.5 = f32[576,512]{1,0:T(8,128)S(1)} collective-permute-done((f32[576,512]{1,0:T(8,128)S(1)}, f32[576,512]{1,0:T(8,128)S(1)}, u32[]{:S(2)}, u32[]{:S(2)}) %collective-permute-start.5) | collective-permute-done | bytes 1179680 | tf_op jit(solution)/shard_map/ppermute | solution.py:13
  347.8 1.6 maximum_bitcast_fusion
  (26 shorter events, 0.8 us)
Async XLA Ops:
  7.2 5.4 %copy-start = (bf16[1,1,128,512]{3,2,1,0:T(8,128)(2,1)S(1)}, bf16[1,1,128,512]{3,2,1,0:T(8,128)(2,1)}, u32[]{:S(2)}) copy-start(bf16[1,1,128,512]{3,2,1,0:T(8,128)(2,1)} %param.14) | copy-start | bytes 393220
  7.2 4.4 %copy-start.6 = (s32[1,1,128]{2,1,0:T(1,128)S(1)}, s32[1,1,128]{2,1,0:T(1,128)}, u32[]{:S(2)}) copy-start(s32[1,1,128]{2,1,0:T(1,128)} %param.13) | copy-start | bytes 1540
  7.2 51.7 %all-gather.2.cloned.1.call-start = ((), (), s32[]{:S(2)}) async-start(), calls=%async_computation | async-start | bytes 2949120 | tf_op jit(solution)/shard_map/all_gather | solution.py:77
  10.6 1.9 copy-start.4
  11.6 143.6 %all-reduce.3.cloned.1.call-start = ((), (), s32[]{:S(2)}) async-start(), calls=%async_computation.1 | async-start | bytes 4718592 | tf_op jit(solution)/shard_map/psum | solution.py:85
  14.0 47.8 %copy-start.3 = (bf16[576,1,1,128]{3,0,2,1:T(8,128)(2,1)S(1)}, bf16[576,1,1,128]{3,0,2,1:T(8,128)(2,1)}, u32[]{:S(2)}) copy-start(bf16[576,1,1,128]{3,0,2,1:T(8,128)(2,1)} %param.12) | copy-start | bytes 442372
  14.0 47.8 %copy-start.5 = (f32[1,1,128]{2,1,0:T(1,128)S(1)}, f32[1,1,128]{2,1,0:T(1,128)}, u32[]{:S(2)}) copy-start(f32[1,1,128]{2,1,0:T(1,128)} %param.10) | copy-start | bytes 1540
  67.9 87.3 %copy-start.1 = (bf16[1,3,512,512]{3,2,1,0:T(8,128)(2,1)S(1)}, bf16[1,3,512,512]{3,2,1,0:T(8,128)(2,1)}, u32[]{:S(2)}) copy-start(bf16[1,3,512,512]{3,2,1,0:T(8,128)(2,1)} %param.15) | copy-start | bytes 4718596
  155.2 5.6 %copy-start.2 = (f32[576,512]{1,0:T(8,128)S(1)}, f32[576,512]{1,0:T(8,128)}, u32[]{:S(2)}) copy-start(f32[576,512]{1,0:T(8,128)} %get-tuple-element.28) | copy-start | bytes 3538948
  157.7 29.9 %collective-permute-start = (f32[576,512]{1,0:T(8,128)S(1)}, f32[576,512]{1,0:T(8,128)S(1)}, u32[]{:S(2)}, u32[]{:S(2)}) collective-permute-start(f32[576,512]{1,0:T(8,128)S(1)} %fusion.15), channel_id=1, source_target_pairs={{0,1},{1,0},{2,3},{3,2},{4,5},{5,4},{6,7},{7,6},{8,9},{9,8},{10,11... | collective-permute-start | bytes 3538952 | tf_op jit(solution)/shard_map/ppermute | solution.py:13
  161.9 51.0 %collective-permute-start.3 = (f32[576,512]{1,0:T(8,128)S(1)}, f32[576,512]{1,0:T(8,128)S(1)}, u32[]{:S(2)}, u32[]{:S(2)}) collective-permute-start(f32[576,512]{1,0:T(8,128)S(1)} %fusion.13), channel_id=1, source_target_pairs={{0,1},{1,0},{2,3},{3,2},{4,5},{5,4},{6,7},{7,6},{8,9},{9,8},{10,11... | collective-permute-start | bytes 3538952 | tf_op jit(solution)/shard_map/ppermute | solution.py:13
  188.7 51.6 %collective-permute-start.1 = (f32[576,512]{1,0:T(8,128)S(1)}, f32[576,512]{1,0:T(8,128)S(1)}, u32[]{:S(2)}, u32[]{:S(2)}) collective-permute-start(f32[576,512]{1,0:T(8,128)S(1)} %fusion.7), channel_id=1, source_target_pairs={{0,2},{1,3},{2,0},{3,1},{4,6},{5,7},{6,4},{7,5},{8,10},{9,11},{10,... | collective-permute-start | bytes 3538952 | tf_op jit(solution)/shard_map/ppermute | solution.py:13
  214.0 50.1 %collective-permute-start.4 = (f32[576,512]{1,0:T(8,128)S(1)}, f32[576,512]{1,0:T(8,128)S(1)}, u32[]{:S(2)}, u32[]{:S(2)}) collective-permute-start(f32[576,512]{1,0:T(8,128)S(1)} %fusion.3), channel_id=1, source_target_pairs={{0,2},{1,3},{2,0},{3,1},{4,6},{5,7},{6,4},{7,5},{8,10},{9,11},{10,... | collective-permute-start | bytes 3538952 | tf_op jit(solution)/shard_map/ppermute | solution.py:13
  241.4 81.1 %collective-permute-start.2 = (f32[576,512]{1,0:T(8,128)S(1)}, f32[576,512]{1,0:T(8,128)S(1)}, u32[]{:S(2)}, u32[]{:S(2)}) collective-permute-start(f32[576,512]{1,0:T(8,128)S(1)} %fusion.5), channel_id=1, source_target_pairs={{0,4},{1,5},{2,6},{3,7},{4,0},{5,1},{6,2},{7,3},{8,12},{9,13},{10,... | collective-permute-start | bytes 3538952 | tf_op jit(solution)/shard_map/ppermute | solution.py:13
  265.3 82.3 %collective-permute-start.5 = (f32[576,512]{1,0:T(8,128)S(1)}, f32[576,512]{1,0:T(8,128)S(1)}, u32[]{:S(2)}, u32[]{:S(2)}) collective-permute-start(f32[576,512]{1,0:T(8,128)S(1)} %fusion.1), channel_id=1, source_target_pairs={{0,4},{1,5},{2,6},{3,7},{4,0},{5,1},{6,2},{7,3},{8,12},{9,13},{10,... | collective-permute-start | bytes 3538952 | tf_op jit(solution)/shard_map/ppermute | solution.py:13
Sparse Core Ops, SparseCore 0:
  11.7 47.2 all-gather.1
  68.1 87.1 all-reduce.2
where the time goes:
time: 357 us; the launch traced here: 356 us
  waiting for transfers between devices  292 us (82%)
  starting transfers between devices  24.8 us (7%)
  matrix products  14.4 us (4%)
  between operations  14.3 us (4%)
  local copies, waits for them, and re-layouts  7.42 us (2%)
  other arithmetic  3.81 us (1%)
    ppermute x6, waiting for transfers between devices, partner(): return lax.ppermute(value, axis, pairs)  159 us
    psum x1, waiting for transfers between devices, shards(): sketch_sum, probe_sum = lax.psum((sketch_part, probe_part), 'blk')  87.3 us
    all_gather x1, waiting for transfers between devices, shards(): piece = lax.all_gather(outgoing, 'blk', axis=1, tiled=True)  44.9 us
    ppermute x6, starting transfers between devices, partner(): return lax.ppermute(value, axis, pairs)  24.7 us
    dot_general x6, matrix products, project(): jnp.dot(current, level_mat.astype(jnp.float32), precision=lax.Precision.H...  7.99 us
  transfers between devices with their start and end apart: 8, of which 8 were waited for; matrix products, arithmetic and copies ran while one was open for 2% of the time, Pallas kernels for 0%

commit v1 on v0

--- a/solution.py
+++ b/solution.py
@@ -74,7 +74,9 @@
         jnp.take(probe_flat, sorting, axis=1), basis_flat, preferred_element_type=jnp.float32
     )
     outgoing = jnp.concatenate([coords, area_row, scaled.astype(jnp.float32)], axis=0)
-    piece = lax.all_gather(outgoing, "blk", axis=1, tiled=True)
+    piece = jnp.concatenate(
+        lax.all_to_all(jnp.stack([outgoing] * lax.axis_size("blk")), "blk", 0, 0), axis=1
+    )
     near_sum = near_block(coords, area_row[0], piece[:3], piece[3], piece[4:].astype(jnp.bfloat16))
     offdiag = (full_sketch.reshape(probe_count, panels).astype(jnp.float32) - near_sum).astype(
         jnp.bfloat16

time: 357 us -> 369 us (1.034)
  starting transfers between devices: 24.8 us -> 34.3 us
  waiting for transfers between devices: 292 us -> 298 us
    all_to_all x0 -> x1, waiting for transfers between devices: none -> 50.3 us  [shards(): lax.all_to_all(jnp.stack([outgoing] * lax.axis_size('blk')), 'blk', 0, 0)]
    all_gather x1 -> x0, waiting for transfers between devices: 44.9 us -> none  [shards(): piece = lax.all_gather(outgoing, 'blk', axis=1, tiled=True)]
    all_to_all x0 -> x1, starting transfers between devices: none -> 9.59 us  [shards(): lax.all_to_all(jnp.stack([outgoing] * lax.axis_size('blk')), 'blk', 0, 0)]
where the time goes in v1:
time: 369 us; the launch traced here: 368 us
  waiting for transfers between devices  298 us (81%)
  starting transfers between devices  34.3 us (9%)
  between operations  14.2 us (4%)
  matrix products  12.3 us (3%)
  local copies, waits for them, and re-layouts  6.4 us (2%)
    ppermute x6, waiting for transfers between devices, partner(): return lax.ppermute(value, axis, pairs)  159 us
    psum x1, waiting for transfers between devices, shards(): sketch_sum, probe_sum = lax.psum((sketch_part, probe_part), 'blk')  88.2 us
    all_to_all x1, waiting for transfers between devices, shards(): lax.all_to_all(jnp.stack([outgoing] * lax.axis_size('blk')), 'blk', 0, 0)  50.3 us
    ppermute x6, starting transfers between devices, partner(): return lax.ppermute(value, axis, pairs)  24.7 us
    all_to_all x1, starting transfers between devices, shards(): lax.all_to_all(jnp.stack([outgoing] * lax.axis_size('blk')), 'blk', 0, 0)  9.59 us
    dot_general x6, matrix products, project(): jnp.dot(current, level_mat.astype(jnp.float32), precision=lax.Precision.H...  7.98 us
  transfers between devices with their start and end apart: 8, of which 8 were waited for; matrix products, arithmetic and copies ran while one was open for 2% of the time, Pallas kernels for 0%

profile of v1, /device:TPU:25, one launch (start us, length us, event | category | flops | bytes accessed | tf_op | source)
XLA Modules:
  0.0 368.1 jit_solution(2840150175996468157)
XLA Ops:
  7.2 1.1 copy.20
  8.3 0.8 copy.19
  9.1 0.8 copy.21
  9.8 0.7 fusion.39
  10.9 1.6 stack.8
  12.5 9.6 %all-to-all-start = ((f32[8,580,128]{2,1,0:T(8,128)}), f32[8,580,128]{2,1,0:T(8,128)S(1)}, u32[]{:S(2)}, u32[]{:S(2)}) async-start(f32[8,580,128]{2,1,0:T(8,128)} %stack.8), calls=%async_computation | async-start | bytes 4784128 | tf_op jit(solution)/shard_map/all_to_all | solution.py:78
  22.2 0.9 gather_fusion.1
  23.1 1.4 fusion.40
  24.5 50.3 %all-to-all-done = f32[8,580,128]{2,1,0:T(8,128)S(1)} async-done(((f32[8,580,128]{2,1,0:T(8,128)}), f32[8,580,128]{2,1,0:T(8,128)S(1)}, u32[]{:S(2)}, u32[]{:S(2)}) %all-to-all-start) | async-done | bytes 2375712 | tf_op jit(solution)/shard_map/all_to_all | solution.py:78
  74.9 1.4 fusion.26
  76.5 0.9 gather_fusion
  77.4 1.5 fusion.42
  78.8 88.2 %all-reduce.3.cloned.1.call-done = (f32[576,512]{1,0:T(8,128)}, f32[576,512]{1,0:T(8,128)}) async-done(((f32[576,512]{1,0:T(8,128)}, f32[576,512]{1,0:T(8,128)}), (f32[576,512]{1,0:T(8,128)}, f32[576,512]{1,0:T(8,128)})) %all-reduce.3.cloned.1.call-update) | async-done | bytes 2359312 | tf_op jit(solution)/shard_map/psum | solution.py:87
  167.0 2.5 fusion.18
  169.5 3.1 collective-permute-start
  172.6 1.1 fusion.16
  173.7 2.2 collective-permute-start.3
  175.9 23.5 %collective-permute-done = f32[576,512]{1,0:T(8,128)S(1)} collective-permute-done((f32[576,512]{1,0:T(8,128)S(1)}, f32[576,512]{1,0:T(8,128)S(1)}, u32[]{:S(2)}, u32[]{:S(2)}) %collective-permute-start) | collective-permute-done | bytes 1179680 | tf_op jit(solution)/shard_map/ppermute | solution.py:13
  199.4 1.1 fusion.10
  200.6 4.6 %collective-permute-start.1 = (f32[576,512]{1,0:T(8,128)S(1)}, f32[576,512]{1,0:T(8,128)S(1)}, u32[]{:S(2)}, u32[]{:S(2)}) collective-permute-start(f32[576,512]{1,0:T(8,128)S(1)} %fusion.10), channel_id=1, source_target_pairs={{0,2},{1,3},{2,0},{3,1},{4,6},{5,7},{6,4},{7,5},{8,10},{9,11},{10,... | collective-permute-start | bytes 3538952 | tf_op jit(solution)/shard_map/ppermute | solution.py:13
  205.2 19.6 %collective-permute-done.3 = f32[576,512]{1,0:T(8,128)S(1)} collective-permute-done((f32[576,512]{1,0:T(8,128)S(1)}, f32[576,512]{1,0:T(8,128)S(1)}, u32[]{:S(2)}, u32[]{:S(2)}) %collective-permute-start.3) | collective-permute-done | bytes 1179680 | tf_op jit(solution)/shard_map/ppermute | solution.py:13
  224.7 1.1 fusion.6
  225.9 4.6 %collective-permute-start.4 = (f32[576,512]{1,0:T(8,128)S(1)}, f32[576,512]{1,0:T(8,128)S(1)}, u32[]{:S(2)}, u32[]{:S(2)}) collective-permute-start(f32[576,512]{1,0:T(8,128)S(1)} %fusion.6), channel_id=1, source_target_pairs={{0,2},{1,3},{2,0},{3,1},{4,6},{5,7},{6,4},{7,5},{8,10},{9,11},{10,... | collective-permute-start | bytes 3538952 | tf_op jit(solution)/shard_map/ppermute | solution.py:13
  230.5 21.7 %collective-permute-done.1 = f32[576,512]{1,0:T(8,128)S(1)} collective-permute-done((f32[576,512]{1,0:T(8,128)S(1)}, f32[576,512]{1,0:T(8,128)S(1)}, u32[]{:S(2)}, u32[]{:S(2)}) %collective-permute-start.1) | collective-permute-done | bytes 1179680 | tf_op jit(solution)/shard_map/ppermute | solution.py:13
  252.1 1.1 fusion.8
  253.2 5.0 %collective-permute-start.2 = (f32[576,512]{1,0:T(8,128)S(1)}, f32[576,512]{1,0:T(8,128)S(1)}, u32[]{:S(2)}, u32[]{:S(2)}) collective-permute-start(f32[576,512]{1,0:T(8,128)S(1)} %fusion.8), channel_id=1, source_target_pairs={{0,4},{1,5},{2,6},{3,7},{4,0},{5,1},{6,2},{7,3},{8,12},{9,13},{10,... | collective-permute-start | bytes 3538952 | tf_op jit(solution)/shard_map/ppermute | solution.py:13
  258.3 17.7 %collective-permute-done.4 = f32[576,512]{1,0:T(8,128)S(1)} collective-permute-done((f32[576,512]{1,0:T(8,128)S(1)}, f32[576,512]{1,0:T(8,128)S(1)}, u32[]{:S(2)}, u32[]{:S(2)}) %collective-permute-start.4) | collective-permute-done | bytes 1179680 | tf_op jit(solution)/shard_map/ppermute | solution.py:13
  276.0 1.1 fusion.4
  277.1 5.2 %collective-permute-start.5 = (f32[576,512]{1,0:T(8,128)S(1)}, f32[576,512]{1,0:T(8,128)S(1)}, u32[]{:S(2)}, u32[]{:S(2)}) collective-permute-start(f32[576,512]{1,0:T(8,128)S(1)} %fusion.4), channel_id=1, source_target_pairs={{0,4},{1,5},{2,6},{3,7},{4,0},{5,1},{6,2},{7,3},{8,12},{9,13},{10,... | collective-permute-start | bytes 3538952 | tf_op jit(solution)/shard_map/ppermute | solution.py:13
  282.3 52.0 %collective-permute-done.2 = f32[576,512]{1,0:T(8,128)S(1)} collective-permute-done((f32[576,512]{1,0:T(8,128)S(1)}, f32[576,512]{1,0:T(8,128)S(1)}, u32[]{:S(2)}, u32[]{:S(2)}) %collective-permute-start.2) | collective-permute-done | bytes 1179680 | tf_op jit(solution)/shard_map/ppermute | solution.py:13
  334.6 24.8 %collective-permute-done.5 = f32[576,512]{1,0:T(8,128)S(1)} collective-permute-done((f32[576,512]{1,0:T(8,128)S(1)}, f32[576,512]{1,0:T(8,128)S(1)}, u32[]{:S(2)}, u32[]{:S(2)}) %collective-permute-start.5) | collective-permute-done | bytes 1179680 | tf_op jit(solution)/shard_map/ppermute | solution.py:13
  359.7 1.6 maximum_bitcast_fusion
  (27 shorter events, 1.1 us)
Async XLA Ops:
  7.2 15.9 %copy-start = (bf16[1,1,128,512]{3,2,1,0:T(8,128)(2,1)S(1)}, bf16[1,1,128,512]{3,2,1,0:T(8,128)(2,1)}, u32[]{:S(2)}) copy-start(bf16[1,1,128,512]{3,2,1,0:T(8,128)(2,1)} %param.14) | copy-start | bytes 393220
  12.5 9.6 %copy-start.6 = (s32[1,1,128]{2,1,0:T(1,128)S(1)}, s32[1,1,128]{2,1,0:T(1,128)}, u32[]{:S(2)}) copy-start(s32[1,1,128]{2,1,0:T(1,128)} %param.13) | copy-start | bytes 1540
  12.5 62.3 %all-to-all-start = ((f32[8,580,128]{2,1,0:T(8,128)}), f32[8,580,128]{2,1,0:T(8,128)S(1)}, u32[]{:S(2)}, u32[]{:S(2)}) async-start(f32[8,580,128]{2,1,0:T(8,128)} %stack.8), calls=%async_computation | async-start | bytes 4784128 | tf_op jit(solution)/shard_map/all_to_all | solution.py:78
  22.1 1.0 copy-start.4
  22.1 144.9 %all-reduce.3.cloned.1.call-start = ((), (), s32[]{:S(2)}) async-start(), calls=%async_computation.1 | async-start | bytes 4718592 | tf_op jit(solution)/shard_map/psum | solution.py:87
  22.2 52.7 %copy-start.3 = (bf16[576,1,1,128]{3,0,2,1:T(8,128)(2,1)S(1)}, bf16[576,1,1,128]{3,0,2,1:T(8,128)(2,1)}, u32[]{:S(2)}) copy-start(bf16[576,1,1,128]{3,0,2,1:T(8,128)(2,1)} %param.12) | copy-start | bytes 442372
  22.2 52.7 %copy-start.5 = (f32[1,1,128]{2,1,0:T(1,128)S(1)}, f32[1,1,128]{2,1,0:T(1,128)}, u32[]{:S(2)}) copy-start(f32[1,1,128]{2,1,0:T(1,128)} %param.10) | copy-start | bytes 1540
  78.8 88.2 %copy-start.1 = (bf16[1,3,512,512]{3,2,1,0:T(8,128)(2,1)S(1)}, bf16[1,3,512,512]{3,2,1,0:T(8,128)(2,1)}, u32[]{:S(2)}) copy-start(bf16[1,3,512,512]{3,2,1,0:T(8,128)(2,1)} %param.15) | copy-start | bytes 4718596
  167.0 5.6 %copy-start.2 = (f32[576,512]{1,0:T(8,128)S(1)}, f32[576,512]{1,0:T(8,128)}, u32[]{:S(2)}) copy-start(f32[576,512]{1,0:T(8,128)} %get-tuple-element.17) | copy-start | bytes 3538948
  169.5 29.9 %collective-permute-start = (f32[576,512]{1,0:T(8,128)S(1)}, f32[576,512]{1,0:T(8,128)S(1)}, u32[]{:S(2)}, u32[]{:S(2)}) collective-permute-start(f32[576,512]{1,0:T(8,128)S(1)} %fusion.18), channel_id=1, source_target_pairs={{0,1},{1,0},{2,3},{3,2},{4,5},{5,4},{6,7},{7,6},{8,9},{9,8},{10,11... | collective-permute-start | bytes 3538952 | tf_op jit(solution)/shard_map/ppermute | solution.py:13
  173.7 51.0 %collective-permute-start.3 = (f32[576,512]{1,0:T(8,128)S(1)}, f32[576,512]{1,0:T(8,128)S(1)}, u32[]{:S(2)}, u32[]{:S(2)}) collective-permute-start(f32[576,512]{1,0:T(8,128)S(1)} %fusion.16), channel_id=1, source_target_pairs={{0,1},{1,0},{2,3},{3,2},{4,5},{5,4},{6,7},{7,6},{8,9},{9,8},{10,11... | collective-permute-start | bytes 3538952 | tf_op jit(solution)/shard_map/ppermute | solution.py:13
  200.6 51.6 %collective-permute-start.1 = (f32[576,512]{1,0:T(8,128)S(1)}, f32[576,512]{1,0:T(8,128)S(1)}, u32[]{:S(2)}, u32[]{:S(2)}) collective-permute-start(f32[576,512]{1,0:T(8,128)S(1)} %fusion.10), channel_id=1, source_target_pairs={{0,2},{1,3},{2,0},{3,1},{4,6},{5,7},{6,4},{7,5},{8,10},{9,11},{10,... | collective-permute-start | bytes 3538952 | tf_op jit(solution)/shard_map/ppermute | solution.py:13
  225.9 50.1 %collective-permute-start.4 = (f32[576,512]{1,0:T(8,128)S(1)}, f32[576,512]{1,0:T(8,128)S(1)}, u32[]{:S(2)}, u32[]{:S(2)}) collective-permute-start(f32[576,512]{1,0:T(8,128)S(1)} %fusion.6), channel_id=1, source_target_pairs={{0,2},{1,3},{2,0},{3,1},{4,6},{5,7},{6,4},{7,5},{8,10},{9,11},{10,... | collective-permute-start | bytes 3538952 | tf_op jit(solution)/shard_map/ppermute | solution.py:13
  253.2 81.1 %collective-permute-start.2 = (f32[576,512]{1,0:T(8,128)S(1)}, f32[576,512]{1,0:T(8,128)S(1)}, u32[]{:S(2)}, u32[]{:S(2)}) collective-permute-start(f32[576,512]{1,0:T(8,128)S(1)} %fusion.8), channel_id=1, source_target_pairs={{0,4},{1,5},{2,6},{3,7},{4,0},{5,1},{6,2},{7,3},{8,12},{9,13},{10,... | collective-permute-start | bytes 3538952 | tf_op jit(solution)/shard_map/ppermute | solution.py:13
  277.1 82.3 %collective-permute-start.5 = (f32[576,512]{1,0:T(8,128)S(1)}, f32[576,512]{1,0:T(8,128)S(1)}, u32[]{:S(2)}, u32[]{:S(2)}) collective-permute-start(f32[576,512]{1,0:T(8,128)S(1)} %fusion.4), channel_id=1, source_target_pairs={{0,4},{1,5},{2,6},{3,7},{4,0},{5,1},{6,2},{7,3},{8,12},{9,13},{10,... | collective-permute-start | bytes 3538952 | tf_op jit(solution)/shard_map/ppermute | solution.py:13
Sparse Core Ops, SparseCore 0:
  79.0 88.0 all-reduce.2
